TPU v7x, 32 devices: a whole 2x2x4 slice. The times are simulated.
32 devices in a mesh: grp: 8 (over z, core), exp: 4 (over y, x).
Axes of the slice: x: 2, y: 2, z: 4, core: 2. Of those that a mesh axis runs over, the one named last changes fastest.
Arguments:
- sky: float32 [32, 6, 8, 512], P(('grp', 'exp')), may hold values from -6 to 6
- observed: bfloat16 [128, 6, 8, 512], P(('grp', 'exp')), may hold values from -6 to 6
- intersections: int32 [128, 4], P(('grp', 'exp')), may hold values from 0 to 7
- resample_index: int32 [128, 4], P(('grp', 'exp')), may hold values from 0 to 7
- psf_index: int32 [128], P(('grp', 'exp')), may hold values from 0 to 15
- resample_table: bfloat16 [8, 512, 512], replicated, may hold values from -0.25 to 0.25
- psf_weights: float32 [16, 8], replicated, may hold values from -5 to 5
- psf_basis: float32 [8, 41], replicated, may hold values from -0.3125 to 0.3125
Outputs:
- sky_out: float32 [32, 6, 8, 512], P(('grp', 'exp'))
- residual: float32 [128, 6, 8, 512], P(('grp', 'exp'))
Inputs may be any that keep to these rules, and one draw needn't show every extreme that they name: `intersections`: with G = 4: an entry v below G names tile v of the exposure's own group; an entry v of G or more names tile v - G of the next group along grp, cyclically.
All inputs are finite; a program needn't handle non-finite values.
Results may differ from a plain program's by a relative error of at most 0.019.
Values may be sent and summed in bfloat16 or wider, within the bound.
A program may use at most 128 MiB of HBM per device.

v0:
```python
import jax
import jax.numpy as jnp
from jax import lax
from jax.sharding import PartitionSpec as P

ITERS = 2


STEP = 0.05


def shifted(block, axis, distance):
    devices = range(lax.axis_size(axis))
    route = [((i - distance) % len(devices), i) for i in devices]
    return lax.ppermute(block, axis, route)


def conv_matrices(kernels, width, taps):
    half = (taps - 1) // 2
    count = kernels.shape[0]
    head = kernels[:, half::-1]
    tail = kernels[:, taps - 1 : half : -1]
    blank = jnp.zeros((count, 2 * width - 1 - taps), jnp.float32)
    pattern = jnp.concatenate([head, blank, tail], axis=1)
    tiled = jnp.broadcast_to(pattern[:, None, :], (count, width, 2 * width - 1)).reshape(
        count, width * (2 * width - 1)
    )
    tiled = tiled[:, : width * (2 * width - 2)].reshape(count, width, 2 * width - 2)[:, :, :width]
    return tiled.astype(jnp.bfloat16)


def fetch_window(sky_half):
    own_group = lax.all_gather(sky_half, "exp", axis=0, tiled=True)
    next_group = shifted(own_group, "grp", -1)
    return jnp.concatenate([own_group, next_group], axis=0)


def return_partials(grads, group_tiles):
    own_part = grads[:group_tiles]
    next_part = grads[group_tiles:]
    arrived = shifted(next_part.astype(jnp.bfloat16), "grp", 1).astype(next_part.dtype)
    return lax.psum_scatter(
        (own_part + arrived).astype(jnp.bfloat16), "exp", scatter_dimension=0, tiled=True
    ).astype(jnp.float32)


def shards(
    sky, observed, intersections, resample_index, psf_index, resample_table, psf_weights, psf_basis
):
    exposures_here, intersection_count = intersections.shape
    group_tiles = sky.shape[0] * lax.axis_size("exp")
    width = resample_table.shape[1]
    taps = psf_basis.shape[1]
    table_rows = psf_weights.shape[0]
    res_count = resample_table.shape[0]
    selector = (
        psf_index[:, None] == lax.broadcasted_iota(jnp.int32, (exposures_here, table_rows), 1)
    ).astype(jnp.float32)
    weights = jnp.sum(selector[:, :, None] * psf_weights[None, :, :], axis=1)
    kernels = jnp.sum(weights[:, :, None] * psf_basis[None, :, :], axis=1)
    conv = conv_matrices(kernels, width, taps)
    window_iota = lax.broadcasted_iota(
        jnp.int32, (exposures_here, intersection_count, 2 * group_tiles), 2
    )
    tile_onehot = intersections[:, :, None] == window_iota
    pick_tiles = tile_onehot.astype(jnp.bfloat16)
    onehots = tile_onehot.astype(jnp.float32)
    res_iota = lax.broadcasted_iota(jnp.int32, (exposures_here, intersection_count, res_count), 2)
    pick_res = (resample_index[:, :, None] == res_iota).astype(jnp.bfloat16)
    matrices = jnp.einsum(
        "ekn,nwv->ekwv", pick_res, resample_table, preferred_element_type=jnp.float32
    ).astype(jnp.bfloat16)
    sky_out = sky
    residual = jnp.zeros(observed.shape, jnp.float32)
    for step in range(ITERS):
        window = fetch_window(sky_out.astype(jnp.bfloat16))
        chosen = jnp.einsum(
            "ekt,tbrw->ekbrw", pick_tiles, window, preferred_element_type=jnp.float32
        ).astype(jnp.bfloat16)
        pre = jnp.zeros(observed.shape, jnp.float32)
        for k in range(intersection_count):
            pre = pre + jnp.einsum(
                "ebrw,ewv->ebrv", chosen[:, k], matrices[:, k], preferred_element_type=jnp.float32
            )
        model = jnp.einsum(
            "ebrw,ewv->ebrv", pre.astype(jnp.bfloat16), conv, preferred_element_type=jnp.float32
        )
        residual = observed.astype(jnp.float32) - model
        back = jnp.einsum(
            "ebrv,ewv->ebrw",
            residual.astype(jnp.bfloat16),
            conv,
            preferred_element_type=jnp.float32,
        ).astype(jnp.bfloat16)
        grads = jnp.zeros((2 * group_tiles,) + observed.shape[1:], jnp.float32)
        for k in range(intersection_count):
            part = jnp.einsum(
                "ebrv,ewv->ebrw", back, matrices[:, k], preferred_element_type=jnp.float32
            )
            grads = grads + jnp.einsum(
                "et,ebrw->tbrw", onehots[:, k], part, precision=lax.Precision.HIGHEST
            )
        sky_out = sky_out + STEP * return_partials(grads, group_tiles)
    return (sky_out, residual)


def solution(mesh):
    in_specs = (
        P(("grp", "exp"), None, None, None),
        P(("grp", "exp"), None, None, None),
        P(("grp", "exp"), None),
        P(("grp", "exp"), None),
        P(("grp", "exp")),
        P(),
        P(),
        P(),
    )
    out_specs = (P(("grp", "exp"), None, None, None), P(("grp", "exp"), None, None, None))
    return jax.shard_map(shards, mesh=mesh, in_specs=in_specs, out_specs=out_specs, check_vma=False)
```

profile of v0, /device:TPU:0, one launch (start us, length us, event | category | flops | bytes accessed | tf_op | source)
XLA Modules:
  0.0 216.9 jit_solution(15102472466168929469)
XLA Ops:
  8.1 10.2 %all_gather.6 = bf16[4,6,8,512]{3,2,1,0:T(8,128)(2,1)S(1)} all-gather(bf16[1,6,8,512]{3,2,1,0:T(8,128)(2,1)S(1)} %convert_element_type.69), channel_id=1, replica_groups=mesh['grp'=8,'exp'=4] {'exp'}, dimensions={0}, use_global_device_ids=true | all-gather | bytes 245760 | tf_op jit(solution)/shard_map/all_gather | solution.py:33
  20.3 10.1 %convolution_convert_fusion = bf16[4,4,512,512]{3,1,2,0:T(4,128)(2,1)} fusion(bf16[8,512,512]{2,1,0:T(8,128)(2,1)} %param.13, s32[4,4]{1,0:T(4,128)} %param.11), kind=kOutput, calls=%fused_computation | convolution fusion | flops 71303296 | bytes 12582976 | tf_op jit(solution)/shard_map/ekn,nwv->ekwv/dot_general | solution.py:70
  30.4 24.7 %fusion.107 = (bf16[4,1,512,512]{3,1,2,0:T(2,128)(2,1)S(1)}, bf16[4,1,512,512]{3,1,2,0:T(2,128)(2,1)S(1)}, bf16[4,1,512,512]{3,1,2,0:T(2,128)(2,1)S(1)}, bf16[4,1,512,512]{3,1,2,0:T(2,128)(2,1)S(1)}) fusion(bf16[4,4,512,512]{3,1,2,0:T(4,128)(2,1)} %convolution_convert_fusion), kind=kLoop, calls=%fused_computation.118 | loop fusion | bytes 16777216 | tf_op jit(solution)/shard_map/slice | solution.py:83
  55.7 1.9 copy.80
  57.6 1.9 copy.84
  59.5 2.0 copy.86
  62.2 2.6 %broadcast_in_dim.5 = bf16[4,512,1023]{2,1,0:T(8,128)(2,1)} broadcast(bf16[4,1023]{1,0:T(4,128)(2,1)S(1)} %maximum_convert_fusion), dimensions={0,2} | broadcast | bytes 4198392 | tf_op jit(solution)/shard_map/broadcast_in_dim | solution.py:25
  64.8 8.5 %reshape.61 = bf16[2095104]{0:T(1024)(128)(2,1)} reshape(bf16[4,512,1023]{2,1,0:T(8,128)(2,1)} %broadcast_in_dim.5) | data formatting | bytes 8380416
  73.3 5.8 %reshape.38 = bf16[4,523776]{1,0:T(4,128)(2,1)} reshape(bf16[2095104]{0:T(1024)(128)(2,1)} %reshape.61) | data formatting | bytes 8380416 | tf_op jit(solution)/shard_map/reshape | solution.py:25
  79.1 5.3 %slice.125 = bf16[4,523264]{1,0:T(4,128)(2,1)} slice(bf16[4,523776]{1,0:T(4,128)(2,1)} %reshape.38), slice={[0:4], [0:523264]} | slice | bytes 8372224 | tf_op jit(solution)/shard_map/slice | solution.py:28
  84.4 5.8 %reshape.63 = bf16[2093056]{0:T(1024)(128)(2,1)} reshape(bf16[4,523264]{1,0:T(4,128)(2,1)} %slice.125) | data formatting | bytes 8372224
  90.3 9.4 %reshape.39 = bf16[4,512,1022]{2,1,0:T(8,128)(2,1)} reshape(bf16[2093056]{0:T(1024)(128)(2,1)} %reshape.63) | data formatting | bytes 8372224 | tf_op jit(solution)/shard_map/reshape | solution.py:28
  100.2 1.7 fusion.109
  106.1 3.3 %convolution_convert_fusion.4 = bf16[4,6,8,512]{3,2,1,0:T(8,128)(2,1)S(1)} fusion(bf16[4,6,8,512]{3,2,1,0:T(8,128)(2,1)S(1)} %fusion.56, bf16[4,512,1022]{2,1,0:T(8,128)(2,1)} %reshape.39, bf16[4,6,8,512]{3,2,1,0:T(8,128)(2,1)S(1)} %copy-done.12), kind=kOutput, calls=%fused_computation.56 | convolution fusion | flops 201719808 | bytes 4775936 | tf_op jit(solution)/shard_map/ebrv,ewv->ebrw/dot_general | solution.py:89
  109.4 2.5 %fusion.30 = f32[4,6,8,512]{3,2,1,0:T(8,128)S(1)} fusion(bf16[4,6,8,512]{3,2,1,0:T(8,128)(2,1)S(1)} %convolution_convert_fusion.4, bf16[4,1,512,512]{3,2,1,0:T(8,128)(2,1)} %copy.80), kind=kOutput, calls=%fused_computation.32 | convolution fusion | flops 100663296 | bytes 2686976 | tf_op jit(solution)/shard_map/ebrv,ewv->ebrw/dot_general | solution.py:97
  117.5 6.9 %collective-permute-done.1 = bf16[4,6,8,512]{3,0,2,1:T(4,128)(2,1)S(1)} collective-permute-done((bf16[4,6,8,512]{3,0,2,1:T(4,128)(2,1)S(1)}, bf16[4,6,8,512]{3,0,2,1:T(4,128)(2,1)S(1)}, u32[]{:S(2)}, u32[]{:S(2)}) %collective-permute-start.1) | collective-permute-done | bytes 196640 | tf_op jit(solution)/shard_map/ppermute | solution.py:15
  125.2 21.6 %reduce-scatter.7.cloned.1.call-done = bf16[1,6,8,512]{3,2,1,0:T(8,128)(2,1)} async-done(((bf16[4,6,8,512]{3,2,1,0:T(8,128)(2,1)}), bf16[1,6,8,512]{3,2,1,0:T(8,128)(2,1)}) %reduce-scatter.7.cloned.1.call-update) | async-done | bytes 49168
  147.7 8.9 %all_gather.7 = bf16[4,6,8,512]{3,2,1,0:T(8,128)(2,1)S(1)} all-gather(bf16[1,6,8,512]{3,2,1,0:T(8,128)(2,1)S(1)} %fusion.97), channel_id=1, replica_groups=mesh['grp'=8,'exp'=4] {'exp'}, dimensions={0}, use_global_device_ids=true | all-gather | bytes 245760 | tf_op jit(solution)/shard_map/all_gather | solution.py:33
  157.2 3.2 %collective-permute-done.2 = bf16[4,6,8,512]{3,0,2,1:T(4,128)(2,1)S(1)} collective-permute-done((bf16[4,6,8,512]{3,0,2,1:T(4,128)(2,1)S(1)}, bf16[4,6,8,512]{3,0,2,1:T(4,128)(2,1)S(1)}, u32[]{:S(2)}, u32[]{:S(2)}) %collective-permute-start.2) | collective-permute-done | bytes 196640 | tf_op jit(solution)/shard_map/ppermute | solution.py:15
  165.0 3.0 %convolution_subtract_fusion = f32[4,6,8,512]{3,2,1,0:T(8,128)S(1)} fusion(f32[4,6,8,512]{3,2,1,0:T(8,128)S(1)} %fusion.43, bf16[4,1,512,512]{3,2,1,0:T(8,128)(2,1)} %copy.86, bf16[4,512,1022]{2,1,0:T(8,128)(2,1)} %reshape.39, bf16[4,6,8,512]{3,2,1,0:T(8,128)(2,1)} %param.9, bf16[4,1,6,8,512]{4,1,3,2,0:T(2,128)(2,1)S(1)} %get-tuple-element.10), kind=kOutput, calls=%fused_computation.50 | convolution fusion | flops 201719808 | bytes 5373952 | tf_op jit(solution)/shard_map/ebrw,ewv->ebrv/dot_general | solution.py:85
  168.0 2.5 %convolution_convert_fusion.3 = bf16[4,6,8,512]{3,2,1,0:T(8,128)(2,1)S(1)} fusion(bf16[4,512,1022]{2,1,0:T(8,128)(2,1)} %reshape.39, f32[4,6,8,512]{3,2,1,0:T(8,128)S(1)} %convolution_subtract_fusion), kind=kOutput, calls=%fused_computation.55 | convolution fusion | flops 100859904 | bytes 2686976 | tf_op jit(solution)/shard_map/ebrv,ewv->ebrw/dot_general | solution.py:89
  170.5 2.3 %fusion.2 = f32[4,6,8,512]{3,2,1,0:T(8,128)S(1)} fusion(bf16[4,6,8,512]{3,2,1,0:T(8,128)(2,1)S(1)} %convolution_convert_fusion.3, bf16[4,1,512,512]{3,2,1,0:T(8,128)(2,1)} %copy.86), kind=kOutput, calls=%fused_computation.4 | convolution fusion | flops 100663296 | bytes 2686976 | tf_op jit(solution)/shard_map/ebrv,ewv->ebrw/dot_general | solution.py:97
  180.1 5.4 %collective-permute-done.3 = bf16[4,6,8,512]{3,0,2,1:T(4,128)(2,1)S(1)} collective-permute-done((bf16[4,6,8,512]{3,0,2,1:T(4,128)(2,1)S(1)}, bf16[4,6,8,512]{3,0,2,1:T(4,128)(2,1)S(1)}, u32[]{:S(2)}, u32[]{:S(2)}) %collective-permute-start.3) | collective-permute-done | bytes 196640 | tf_op jit(solution)/shard_map/ppermute | solution.py:15
  186.3 22.3 %reduce-scatter.9.cloned.1.call-done = bf16[1,6,8,512]{3,2,1,0:T(8,128)(2,1)} async-done(((bf16[4,6,8,512]{3,2,1,0:T(8,128)(2,1)}), bf16[1,6,8,512]{3,2,1,0:T(8,128)(2,1)}) %reduce-scatter.9.cloned.1.call-update) | async-done | bytes 49168
  (88 shorter events, 30.6 us)
Async XLA Ops:
  7.2 139.7 %reduce-scatter.7.cloned.1.call-start = ((), (), s32[]{:S(2)}) async-start(), calls=%async_computation.2 | async-start | bytes 245760
  18.4 81.3 %collective-permute-start = (bf16[4,6,8,512]{3,0,2,1:T(4,128)(2,1)S(1)}, bf16[4,6,8,512]{3,0,2,1:T(4,128)(2,1)S(1)}, u32[]{:S(2)}, u32[]{:S(2)}) collective-permute-start(bf16[4,6,8,512]{3,0,2,1:T(4,128)(2,1)S(1)} %copy.47), channel_id=1, source_target_pairs={{4,0},{8,4},{12,8},{16,12},{20,16},{24,20},{28,24},{0,28},{5,1},{9... | collective-permute-start | bytes 589832 | tf_op jit(solution)/shard_map/ppermute | solution.py:15
  59.5 2.0 copy-start.15
  59.5 2.0 copy-start.14
  59.5 2.1 copy-start.13
  101.9 1.6 copy-start
  102.4 1.9 copy-start.3
  104.0 1.7 copy-start.7
  104.7 1.4 copy-start.12
  109.4 3.2 %copy-start.4 = (bf16[4,1,512,512]{3,2,1,0:T(8,128)(2,1)S(1)}, bf16[4,1,512,512]{3,2,1,0:T(8,128)(2,1)}, u32[]{:S(2)}) copy-start(bf16[4,1,512,512]{3,2,1,0:T(8,128)(2,1)} %copy.84) | copy-start | bytes 6291460
  111.9 1.6 copy-start.8
  116.5 30.3 %copy-start.10 = (f32[1,6,8,512]{3,2,1,0:T(8,128)S(1)}, f32[1,6,8,512]{3,2,1,0:T(8,128)}, u32[]{:S(2)}) copy-start(f32[1,6,8,512]{3,2,1,0:T(8,128)} %param.8) | copy-start | bytes 294916
  117.4 6.9 %collective-permute-start.1 = (bf16[4,6,8,512]{3,0,2,1:T(4,128)(2,1)S(1)}, bf16[4,6,8,512]{3,0,2,1:T(4,128)(2,1)S(1)}, u32[]{:S(2)}, u32[]{:S(2)}) collective-permute-start(bf16[4,6,8,512]{3,0,2,1:T(4,128)(2,1)S(1)} %slice.164), channel_id=1, source_target_pairs={{28,0},{0,4},{4,8},{8,12},{12,16},{16,20},{20,24},{24,28},{29,1},{... | collective-permute-start | bytes 589832 | tf_op jit(solution)/shard_map/ppermute | solution.py:15
  125.2 83.4 %reduce-scatter.9.cloned.1.call-start = ((), (), s32[]{:S(2)}) async-start(), calls=%async_computation.3 | async-start | bytes 245760
  156.7 3.6 %collective-permute-start.2 = (bf16[4,6,8,512]{3,0,2,1:T(4,128)(2,1)S(1)}, bf16[4,6,8,512]{3,0,2,1:T(4,128)(2,1)S(1)}, u32[]{:S(2)}, u32[]{:S(2)}) collective-permute-start(bf16[4,6,8,512]{3,0,2,1:T(4,128)(2,1)S(1)} %copy.56), channel_id=1, source_target_pairs={{4,0},{8,4},{12,8},{16,12},{20,16},{24,20},{28,24},{0,28},{5,1},{9... | collective-permute-start | bytes 589832 | tf_op jit(solution)/shard_map/ppermute | solution.py:15
  162.2 1.6 copy-start.1
  162.6 1.9 copy-start.5
  168.0 4.8 %copy-start.9 = (f32[4,6,8,512]{3,2,1,0:T(8,128)}, f32[4,6,8,512]{3,2,1,0:T(8,128)S(1)}, u32[]{:S(2)}) copy-start(f32[4,6,8,512]{3,2,1,0:T(8,128)S(1)} %convolution_subtract_fusion) | copy-start | bytes 1179652
  168.0 4.8 %copy-start.6 = (bf16[4,1,512,512]{3,2,1,0:T(8,128)(2,1)S(1)}, bf16[4,1,512,512]{3,2,1,0:T(8,128)(2,1)}, u32[]{:S(2)}) copy-start(bf16[4,1,512,512]{3,2,1,0:T(8,128)(2,1)} %copy.84) | copy-start | bytes 6291460
  172.9 1.6 copy-start.2
  177.5 31.1 %copy-start.11 = (bf16[1,6,8,512]{3,2,1,0:T(8,128)(2,1)S(1)}, bf16[1,6,8,512]{3,2,1,0:T(8,128)(2,1)}, u32[]{:S(2)}) copy-start(bf16[1,6,8,512]{3,2,1,0:T(8,128)(2,1)} %reduce-scatter.7.cloned.1.call-done) | copy-start | bytes 147460
  178.4 7.1 %collective-permute-start.3 = (bf16[4,6,8,512]{3,0,2,1:T(4,128)(2,1)S(1)}, bf16[4,6,8,512]{3,0,2,1:T(4,128)(2,1)S(1)}, u32[]{:S(2)}, u32[]{:S(2)}) collective-permute-start(bf16[4,6,8,512]{3,0,2,1:T(4,128)(2,1)S(1)} %slice.163), channel_id=1, source_target_pairs={{28,0},{0,4},{4,8},{8,12},{12,16},{16,20},{20,24},{24,28},{29,1},{... | collective-permute-start | bytes 589832 | tf_op jit(solution)/shard_map/ppermute | solution.py:15
Sparse Core Ops, SparseCore 0:
  125.3 21.4 reduce-scatter.6
  186.5 22.0 reduce-scatter.8
where the time goes:
time: 218 us; the launch traced here: 217 us
  local copies, waits for them, and re-layouts  78.7 us (36%)
  waiting for transfers between devices  59.4 us (27%)
  matrix products  38.2 us (18%)
  blocking collectives  19.1 us (9%)
  between operations  14.5 us (7%)
  other arithmetic  3.8 us (2%)
  starting transfers between devices  3.34 us (2%)
    unnamed x4, waiting for transfers between devices  43.9 us
    unnamed x39, local copies, waits for them, and re-layouts  25.5 us
    slice x1, local copies, waits for them, and re-layouts, shards(): matrices[:, k]  24.7 us
    all_gather x2, blocking collectives, fetch_window(): own_group = lax.all_gather(sky_half, 'exp', axis=0, tiled=True)  19.1 us
    ppermute x4, waiting for transfers between devices, shifted(): return lax.ppermute(block, axis, route)  15.5 us
    dot_general x1, matrix products, shards(): jnp.einsum('ekn,nwv->ekwv', pick_res, resample_table, preferred_element_t...  10.1 us
    reshape x1, local copies, waits for them, and re-layouts, conv_matrices(): tiled[:, :width * (2 * width - 2)].reshape(count, width, 2 * width - 2)  9.37 us
    dot_general x8, matrix products, shards(): jnp.einsum('ebrv,ewv->ebrw', back, matrices[:, k], preferred_element_type...  9.1 us
  transfers between devices with their start and end apart: 6, of which 5 were waited for; matrix products, arithmetic and copies ran while one was open for 37% of the time, Pallas kernels for 0%

commit v1 on v0

v1 whole, which is shorter than its diff:
```python
import functools

import jax
import jax.numpy as jnp
from jax import lax
from jax.experimental import pallas as pl
from jax.experimental.pallas import tpu as pltpu
from jax.sharding import PartitionSpec as P

ITERS = 2
STEP = 0.05
LANES = 128
MESH = pl.DeviceIdType.MESH
NN = (((1,), (0,)), ((), ()))
NT = (((1,), (1,)), ((), ()))


def dot(a, b, dims):
    return lax.dot_general(a, b, dims, preferred_element_type=jnp.float32)


def build_conv(psf_smem, weights_smem, basis_ref, taps_buf, conv_t):
    count, width, _ = conv_t.shape
    comp, taps = basis_ref.shape
    half = (taps - 1) // 2
    taps_buf[...] = jnp.zeros_like(taps_buf)
    taps_buf[:, : taps - half] = basis_ref[:, half:]
    taps_buf[:, 2 * LANES - half :] = basis_ref[:, :half]
    rows = lax.broadcasted_iota(jnp.int32, (LANES, LANES), 0)
    cols = lax.broadcasted_iota(jnp.int32, (LANES, LANES), 1)
    blank = jnp.zeros((LANES, LANES), jnp.bfloat16)
    blocks = width // LANES
    for e in range(count):
        kern = jnp.zeros((1, 2 * LANES), jnp.float32)
        for c in range(comp):
            kern = kern + weights_smem[psf_smem[e], c] * taps_buf[c : c + 1, :]
        wide = jnp.broadcast_to(kern, (LANES, 2 * LANES))
        rolled = pltpu.roll(wide, 0, 1, stride=1, stride_axis=0)
        edge = rolled[:, LANES:]
        diagonal = rolled[:, :LANES].astype(jnp.bfloat16)
        right = jnp.where(cols < rows, edge, 0.0).astype(jnp.bfloat16)
        left = jnp.where(cols > rows, edge, 0.0).astype(jnp.bfloat16)
        for i in range(blocks):
            for j in range(blocks):
                block = {0: diagonal, 1: right, -1: left}.get(j - i, blank)
                conv_t[e, i * LANES : (i + 1) * LANES, j * LANES : (j + 1) * LANES] = block


def kernel(
    n_grp, n_exp, tile_smem, res_smem, psf_smem, weights_smem, basis_ref, sky_ref, obs_ref, table_hbm,
    sky_out, resid_out,
    table, window, outbox, inbox, parts, conv_t, taps_buf,
    table_sem, fwd_send, fwd_recv, bwd_send, bwd_recv,
):
    g = lax.axis_index("grp")
    x = lax.axis_index("exp")
    before = lax.rem(g + n_grp - 1, n_grp)
    after = lax.rem(g + 1, n_grp)
    count, picks = tile_smem.shape

    load = pltpu.make_async_copy(table_hbm, table, table_sem)
    load.start()
    window[0, x] = sky_ref[...].astype(jnp.bfloat16)
    sky_out[...] = sky_ref[...]

    barrier = pltpu.get_barrier_semaphore()
    for j in range(n_exp):
        peer = lax.rem(x + j, n_exp)
        for group in (before, g, after):
            if j or group is not g:
                pl.semaphore_signal(barrier, inc=1, device_id=(group, peer), device_id_type=MESH)
    pl.semaphore_wait(barrier, 3 * n_exp - 1)

    def send(src, dst, send_sem, recv_sem, where):
        copy = pltpu.make_async_remote_copy(
            src_ref=src, dst_ref=dst, send_sem=send_sem, recv_sem=recv_sem, device_id=where, device_id_type=MESH
        )
        copy.start()
        return copy

    def spread(step):
        copies = []
        for j in range(n_exp):
            peer = lax.rem(x + j, n_exp)
            copies.append(send(
                window.at[step, x], window.at[step, n_exp + x], fwd_send.at[step, n_exp + j],
                fwd_recv.at[step, n_exp + x], (before, peer),
            ))
            if j:
                copies.append(send(
                    window.at[step, x], window.at[step, x], fwd_send.at[step, j], fwd_recv.at[step, x], (g, peer)
                ))
        return copies

    def arrive(buf, sem, step, slot):
        pltpu.make_async_copy(buf.at[step, slot], buf.at[step, slot], sem.at[step, slot]).wait()

    pending = spread(0)
    build_conv(psf_smem, weights_smem, basis_ref, taps_buf, conv_t)
    load.wait()

    for step in range(ITERS):
        for j in range(1, n_exp):
            arrive(window, fwd_recv, step, lax.rem(x + j, n_exp))
        for j in range(n_exp):
            arrive(window, fwd_recv, step, n_exp + j)

        for e in range(count):
            pre = dot(window[step, tile_smem[e, 0]], table[res_smem[e, 0]], NN)
            for k in range(1, picks):
                pre = pre + dot(window[step, tile_smem[e, k]], table[res_smem[e, k]], NN)
            model = dot(pre.astype(jnp.bfloat16), conv_t[e], NT)
            residual = obs_ref[e].astype(jnp.float32) - model
            if step == ITERS - 1:
                resid_out[e] = residual
            back = dot(residual.astype(jnp.bfloat16), conv_t[e], NN).astype(jnp.bfloat16)
            for k in range(picks):
                parts[e, k] = dot(back, table[res_smem[e, k]], NT)

        def gather(tile):
            total = jnp.zeros(sky_ref.shape, jnp.float32)
            for e in range(count):
                for k in range(picks):
                    keep = jnp.where(tile_smem[e, k] == tile, jnp.float32(1.0), jnp.float32(0.0))
                    total = total + keep * parts[e, k]
            return total

        for j in range(n_exp):
            peer = lax.rem(x + j, n_exp)
            outbox[step, n_exp + peer] = gather(n_exp + peer).astype(jnp.bfloat16)
            pending.append(send(
                outbox.at[step, n_exp + peer], inbox.at[step, n_exp + x], bwd_send.at[step, n_exp + j],
                bwd_recv.at[step, n_exp + x], (after, peer),
            ))
            if j:
                outbox[step, peer] = gather(peer).astype(jnp.bfloat16)
                pending.append(send(
                    outbox.at[step, peer], inbox.at[step, x], bwd_send.at[step, j], bwd_recv.at[step, x], (g, peer)
                ))
        total = gather(x)
        for j in range(1, n_exp):
            slot = lax.rem(x + j, n_exp)
            arrive(inbox, bwd_recv, step, slot)
            total = total + inbox[step, slot].astype(jnp.float32)
        for j in range(n_exp):
            slot = n_exp + j
            arrive(inbox, bwd_recv, step, slot)
            total = total + inbox[step, slot].astype(jnp.float32)
        updated = sky_out[...] + STEP * total
        sky_out[...] = updated
        if step < ITERS - 1:
            window[step + 1, x] = updated.astype(jnp.bfloat16)
            pending += spread(step + 1)

    for copy in pending:
        copy.wait_send()


def shards(
    n_grp, n_exp, sky, observed, intersections, resample_index, psf_index, resample_table, psf_weights, psf_basis
):
    tiles, bands, rows, width = sky.shape
    count, picks = intersections.shape
    flat = tiles * bands * rows
    slots = 2 * n_exp
    comp = psf_basis.shape[0]
    smem = pl.BlockSpec(memory_space=pltpu.SMEM)
    vmem = pl.BlockSpec(memory_space=pltpu.VMEM)
    sky_out, residual = pl.pallas_call(
        functools.partial(kernel, n_grp, n_exp),
        out_shape=(
            jax.ShapeDtypeStruct((flat, width), jnp.float32),
            jax.ShapeDtypeStruct((count, flat, width), jnp.float32),
        ),
        in_specs=[smem] * 4 + [vmem] * 3 + [pl.BlockSpec(memory_space=pl.ANY)],
        out_specs=(vmem, vmem),
        scratch_shapes=[
            pltpu.VMEM(resample_table.shape, jnp.bfloat16),
            pltpu.VMEM((ITERS, slots, flat, width), jnp.bfloat16),
            pltpu.VMEM((ITERS, slots, flat, width), jnp.bfloat16),
            pltpu.VMEM((ITERS, slots, flat, width), jnp.bfloat16),
            pltpu.VMEM((count, picks, flat, width), jnp.float32),
            pltpu.VMEM((count, width, width), jnp.bfloat16),
            pltpu.VMEM((comp, 2 * LANES), jnp.float32),
            pltpu.SemaphoreType.DMA,
        ]
        + [pltpu.SemaphoreType.DMA((ITERS, slots))] * 4,
        compiler_params=pltpu.CompilerParams(
            collective_id=0, has_side_effects=True, vmem_limit_bytes=48 * 2**20
        ),
    )(
        intersections, resample_index, psf_index, psf_weights, psf_basis,
        sky.reshape(flat, width), observed.reshape(count, flat, width), resample_table,
    )
    return sky_out.reshape(sky.shape), residual.reshape(observed.shape)


def solution(mesh):
    both = ("grp", "exp")
    in_specs = (
        P(both, None, None, None), P(both, None, None, None), P(both, None), P(both, None), P(both), P(), P(), P(),
    )
    out_specs = (P(both, None, None, None), P(both, None, None, None))
    body = functools.partial(shards, mesh.shape["grp"], mesh.shape["exp"])
    return jax.shard_map(body, mesh=mesh, in_specs=in_specs, out_specs=out_specs, check_vma=False)
```

time: 218 us -> 52.3 us (0.24)
  local copies, waits for them, and re-layouts: 78.7 us -> 8.86 us
  waiting for transfers between devices: 59.4 us -> 0 us
  Pallas kernels: 0 us -> 42.4 us
  matrix products: 38.2 us -> 0 us
  blocking collectives: 19.1 us -> 0 us
  between operations: 14.5 us -> 0.65 us
  other arithmetic: 3.8 us -> 0 us
  starting transfers between devices: 3.34 us -> 0 us
    unnamed x4 -> x0, waiting for transfers between devices: 43.9 us -> none
    pallas_call x0 -> x1, Pallas kernels: none -> 42.4 us  [shards(): pl.pallas_call(functools.partial(kernel, n_grp, n_exp), out_shape=(jax.Sh...]
    dot_general x29 -> x0, matrix products: 38.2 us -> none  [the longest x1 10.1 us: shards(): jnp.einsum('ekn,nwv->ekwv', pick_res, resample_table, preferred_element_t...]
    slice x7 -> x0, local copies, waits for them, and re-layouts: 33.3 us -> none  [the longest x1 24.7 us: shards(): matrices[:, k]]
    all_gather x2 -> x0, blocking collectives: 19.1 us -> none  [fetch_window(): own_group = lax.all_gather(sky_half, 'exp', axis=0, tiled=True)]
    unnamed x39 -> x17, local copies, waits for them, and re-layouts: 25.5 us -> 8.86 us
    ppermute x4 -> x0, waiting for transfers between devices: 15.5 us -> none  [shifted(): return lax.ppermute(block, axis, route)]
    reshape x2 -> x0, local copies, waits for them, and re-layouts: 15.2 us -> none  [the longest x1 9.37 us: conv_matrices(): tiled[:, :width * (2 * width - 2)].reshape(count, width, 2 * width - 2)]
  transfers between devices with their start and end apart: 6 -> 0, of which waited for: 5 -> 0; matrix products, arithmetic and copies ran while one was open for 37% -> 0% of each run, Pallas kernels for 0% -> 0%
where the time goes in v1:
time: 52.3 us; the launch traced here: 51.9 us
  Pallas kernels  42.4 us (81%)
  local copies, waits for them, and re-layouts  8.86 us (17%)
  between operations  0.65 us (1%)
    pallas_call x1, Pallas kernels, shards(): pl.pallas_call(functools.partial(kernel, n_grp, n_exp), out_shape=(jax.Sh...  42.4 us
    unnamed x17, local copies, waits for them, and re-layouts  8.86 us

profile of v1, /device:TPU:0, one launch (start us, length us, event | category | flops | bytes accessed | tf_op | source)
XLA Modules:
  0.0 51.9 jit_solution(11415782428891302961)
XLA Ops:
  0.6 0.8 %copy.10.weights_smem = f32[16,8]{1,0:T(8,128)S(1)} copy(f32[16,8]{0,1:T(8,128)} %param.14) | data formatting | bytes 1024 | tf_op args[6]
  1.4 0.0 copy-start
  1.4 2.2 %copy-done = bf16[8,512,512]{2,1,0:T(8,128)(2,1)S(1)} copy-done((bf16[8,512,512]{2,1,0:T(8,128)(2,1)S(1)}, bf16[8,512,512]{2,1,0:T(8,128)(2,1)}, u32[]{:S(2)}) %copy-start) | copy-done | bytes 4194328
  3.6 0.0 copy-start.1
  3.6 0.9 %copy-done.1 = bf16[4,6,8,512]{3,2,1,0:T(8,128)(2,1)S(1)} copy-done((bf16[4,6,8,512]{3,2,1,0:T(8,128)(2,1)S(1)}, bf16[4,6,8,512]{3,2,1,0:T(8,128)(2,1)}, u32[]{:S(2)}) %copy-start.1) | copy-done | bytes 196632
  4.5 0.0 copy-start.2
  4.5 0.9 %copy-done.2 = f32[1,6,8,512]{3,2,1,0:T(8,128)S(1)} copy-done((f32[1,6,8,512]{3,2,1,0:T(8,128)S(1)}, f32[1,6,8,512]{3,2,1,0:T(8,128)}, u32[]{:S(2)}) %copy-start.2) | copy-done | bytes 98328
  5.4 0.0 copy-start.3
  5.4 0.7 %copy-done.3 = f32[8,41]{1,0:T(8,128)S(1)} copy-done((f32[8,41]{1,0:T(8,128)S(1)}, f32[8,41]{1,0:T(8,128)}, u32[]{:S(2)}) %copy-start.3) | copy-done | bytes 1336
  6.1 0.0 copy-start.4
  6.1 0.7 %copy-done.4 = s32[4,4]{1,0:T(4,128)S(1)} copy-done((s32[4,4]{1,0:T(4,128)S(1)}, s32[4,4]{1,0:T(4,128)}, u32[]{:S(2)}) %copy-start.4) | copy-done | bytes 88
  6.8 0.0 copy-start.5
  6.8 0.7 %copy-done.5 = s32[4,4]{1,0:T(4,128)S(1)} copy-done((s32[4,4]{1,0:T(4,128)S(1)}, s32[4,4]{1,0:T(4,128)}, u32[]{:S(2)}) %copy-start.5) | copy-done | bytes 88
  7.4 0.0 copy-start.6
  7.5 0.7 %copy-done.6 = s32[4]{0:T(128)S(1)} copy-done((s32[4]{0:T(128)S(1)}, s32[4]{0:T(128)}, u32[]{:S(2)}) %copy-start.6) | copy-done | bytes 40
  8.1 42.4 %shard_map.95 = (f32[48,512]{1,0:T(8,128)S(1)}, f32[4,48,512]{2,1,0:T(8,128)S(1)}) custom-call(s32[4,4]{1,0:T(4,128)S(1)} %copy-done.4, s32[4,4]{1,0:T(4,128)S(1)} %copy-done.5, s32[4]{0:T(128)S(1)} %copy-done.6, f32[16,8]{1,0:T(8,128)S(1)} %copy.10.weights_smem, f32[8,41]{1,0:T(8,128)S(1)} %copy-done.3, f32[48,512]{1,0:T(8,128)S(1)} %bitcast.7, ...), custom_call_target="tpu_custom_call" | custom-call | tf_op jit(solution)/shard_map/pallas_call | solution.py:169
  50.6 0.6 %copy.13 = f32[1,6,8,512]{3,2,1,0:T(8,128)} copy(f32[1,6,8,512]{3,2,1,0:T(8,128)S(1)} %bitcast.6) | data formatting | bytes 196608
  51.2 0.7 %copy.14 = f32[4,6,8,512]{3,2,1,0:T(8,128)} copy(f32[4,6,8,512]{3,2,1,0:T(8,128)S(1)} %bitcast.4) | data formatting | bytes 786432
Async XLA Ops:
  1.4 2.2 %copy-start = (bf16[8,512,512]{2,1,0:T(8,128)(2,1)S(1)}, bf16[8,512,512]{2,1,0:T(8,128)(2,1)}, u32[]{:S(2)}) copy-start(bf16[8,512,512]{2,1,0:T(8,128)(2,1)} %table_hbm.1) | copy-start | bytes 12582916
  3.6 0.9 %copy-start.1 = (bf16[4,6,8,512]{3,2,1,0:T(8,128)(2,1)S(1)}, bf16[4,6,8,512]{3,2,1,0:T(8,128)(2,1)}, u32[]{:S(2)}) copy-start(bf16[4,6,8,512]{3,2,1,0:T(8,128)(2,1)} %param.9) | copy-start | bytes 589828
  4.5 0.9 %copy-start.2 = (f32[1,6,8,512]{3,2,1,0:T(8,128)S(1)}, f32[1,6,8,512]{3,2,1,0:T(8,128)}, u32[]{:S(2)}) copy-start(f32[1,6,8,512]{3,2,1,0:T(8,128)} %param.8) | copy-start | bytes 294916
  5.4 0.7 %copy-start.3 = (f32[8,41]{1,0:T(8,128)S(1)}, f32[8,41]{1,0:T(8,128)}, u32[]{:S(2)}) copy-start(f32[8,41]{1,0:T(8,128)} %basis_ref.1) | copy-start | bytes 3940
  6.1 0.7 %copy-start.4 = (s32[4,4]{1,0:T(4,128)S(1)}, s32[4,4]{1,0:T(4,128)}, u32[]{:S(2)}) copy-start(s32[4,4]{1,0:T(4,128)} %tile_smem.1) | copy-start | bytes 196
  6.8 0.7 %copy-start.5 = (s32[4,4]{1,0:T(4,128)S(1)}, s32[4,4]{1,0:T(4,128)}, u32[]{:S(2)}) copy-start(s32[4,4]{1,0:T(4,128)} %res_smem.1) | copy-start | bytes 196
  7.4 0.7 %copy-start.6 = (s32[4]{0:T(128)S(1)}, s32[4]{0:T(128)}, u32[]{:S(2)}) copy-start(s32[4]{0:T(128)} %psf_smem.1) | copy-start | bytes 52

commit v2 on v1

v2 whole, which is shorter than its diff:
```python
import functools

import jax
import jax.numpy as jnp
from jax import lax
from jax.experimental import pallas as pl
from jax.experimental.pallas import tpu as pltpu
from jax.sharding import PartitionSpec as P

ITERS = 2
STEP = 0.05
LANES = 128
PAD = 64
MESH = pl.DeviceIdType.MESH
NN = (((1,), (0,)), ((), ()))
NT = (((1,), (1,)), ((), ()))


def dot(a, b, dims):
    return lax.dot_general(a, b, dims, preferred_element_type=jnp.float32)


def pad_rows(value, rows):
    short = rows - value.shape[0]
    if not short:
        return value
    return jnp.concatenate([value, jnp.zeros((short, value.shape[1]), value.dtype)], axis=0)


def put(ref, start, value):
    for c in range(ref.shape[0]):
        ref[c, start : start + value.shape[0], :] = value[:, c * LANES : (c + 1) * LANES]


def every(ref, start, size, stride):
    return jnp.concatenate([ref[c, pl.ds(start, size, stride=stride), :] for c in range(ref.shape[0])], axis=1)


def banded(value, band, dims):
    rows, width = value.shape
    blocks = width // LANES
    wide = jnp.concatenate([value, jnp.zeros((rows, 2 * PAD), jnp.float32)], axis=1)
    wide = pltpu.roll(wide, PAD, 1).astype(jnp.bfloat16)
    stacked = jnp.concatenate([wide[:, j * LANES : (j + 2) * LANES] for j in range(blocks)], axis=0)
    out = dot(stacked, band, dims)
    return jnp.concatenate([out[j * rows : (j + 1) * rows] for j in range(blocks)], axis=1)


def kernel(n_grp, n_exp, *refs):
    sources, (sky_out, resid_out), held, rest = refs[:8], refs[8:10], refs[10:18], refs[18:]
    tile_smem, res_smem, psf_smem, weights_smem, basis_ref, sky_ref, obs_ref, table = held
    (load_sem, sky_stage, obs_stage, meta, win, obs, back_in, grad_in, grad_out, delta_stage, delta_in,
     res_stage, res_in, taps, wide, mixed, pre, back, folded, grad, state, delta, pick_f, pick_b, band_f, band_b,
     sky_send, sky_recv, meta_send, meta_recv, obs_send, obs_recv, hop_send, hop_recv, grad_send, grad_recv,
     delta_send, delta_recv, res_send, res_recv) = rest
    g = lax.axis_index("grp")
    x = lax.axis_index("exp")
    before = lax.rem(g + n_grp - 1, n_grp)
    after = lax.rem(g + 1, n_grp)
    count, picks = tile_smem.shape
    flat, width = sky_ref.shape
    mats = table.shape[0]
    comp, tap_count = basis_ref.shape
    half = (tap_count - 1) // 2
    rows = flat // n_exp
    padded = sky_stage.shape[1]
    group_exp = count * n_exp
    tiles = 2 * n_exp

    loads = [pltpu.make_async_copy(src, dst, load_sem.at[i]) for i, (src, dst) in enumerate(zip(sources, held))]
    for i in (5, 0, 1, 2, 3, 4, 6, 7):
        loads[i].start()

    barrier = pltpu.get_barrier_semaphore()
    for j in range(1, n_exp):
        pl.semaphore_signal(barrier, inc=1, device_id=(g, lax.rem(x + j, n_exp)), device_id_type=MESH)
    for group in (before, after):
        pl.semaphore_signal(barrier, inc=1, device_id=(group, x), device_id_type=MESH)

    def send(src, dst, send_sem, recv_sem, where):
        copy = pltpu.make_async_remote_copy(
            src_ref=src, dst_ref=dst, send_sem=send_sem, recv_sem=recv_sem, device_id=where, device_id_type=MESH
        )
        copy.start()
        pending.append(copy)

    def arrive(ref, sem):
        pltpu.make_async_copy(ref, ref, sem).wait()

    pending = []
    loads[5].wait()
    for p in range(n_exp):
        sky_stage[p] = pad_rows(sky_ref[p * rows : (p + 1) * rows, :], padded).astype(jnp.bfloat16)
    win[0, x] = sky_stage[x]
    pl.semaphore_wait(barrier, n_exp + 1)
    for j in range(1, n_exp):
        peer = lax.rem(x + j, n_exp)
        send(sky_stage.at[peer], win.at[0, x], sky_send.at[j], sky_recv.at[x], (g, peer))

    for i in (0, 1, 2, 3, 4):
        loads[i].wait()
    taps[...] = jnp.zeros_like(taps)
    taps[:, PAD - half : PAD - half + tap_count] = basis_ref[...]
    lane = lax.broadcasted_iota(jnp.int32, (1, LANES), 1)
    info = []
    for e in range(count):
        fields = jnp.zeros((1, LANES), jnp.float32)
        for k in range(picks):
            fields = jnp.where(lane == k, tile_smem[e, k].astype(jnp.float32), fields)
            fields = jnp.where(lane == picks + k, res_smem[e, k].astype(jnp.float32), fields)
        kern = jnp.zeros((1, 2 * LANES), jnp.float32)
        for c in range(comp):
            kern = kern + weights_smem[c, psf_smem[e]] * taps[c : c + 1, :]
        info.append(jnp.concatenate([fields, kern], axis=1))
    meta[x] = pad_rows(jnp.concatenate(info, axis=0), meta.shape[1])
    for j in range(1, n_exp):
        peer = lax.rem(x + j, n_exp)
        send(meta.at[x], meta.at[x], meta_send.at[j], meta_recv.at[x], (g, peer))

    loads[6].wait()
    for e in range(count):
        whole = obs_ref[e].astype(jnp.float32)
        for p in range(n_exp):
            obs_stage[p, e] = pad_rows(whole[p * rows : (p + 1) * rows, :], padded).astype(jnp.bfloat16)
    obs[x] = obs_stage[x]
    for j in range(1, n_exp):
        peer = lax.rem(x + j, n_exp)
        send(obs_stage.at[peer], obs.at[x], obs_send.at[j], obs_recv.at[x], (g, peer))

    def hop(step):
        send(
            win.at[step, pl.ds(0, n_exp)], win.at[step, pl.ds(n_exp, n_exp)], hop_send.at[step], hop_recv.at[step],
            (before, x),
        )

    for j in range(1, n_exp):
        slot = lax.rem(x + j, n_exp)
        arrive(win.at[0, slot], sky_recv.at[slot])
    hop(0)
    for t in range(n_exp):
        state[t] = win[0, t].astype(jnp.float32)
        delta[t] = jnp.zeros_like(state[t])

    for j in range(1, n_exp):
        slot = lax.rem(x + j, n_exp)
        arrive(meta.at[slot], meta_recv.at[slot])
    info = jnp.concatenate([meta[d, :count, :] for d in range(n_exp)], axis=0)
    fields = info[:, :LANES]
    tile_lane = lax.broadcasted_iota(jnp.int32, (group_exp, LANES), 1).astype(jnp.float32)
    columns = [jnp.broadcast_to(fields[:, k : k + 1], (group_exp, LANES)) for k in range(2 * picks)]
    across = jnp.transpose(pad_rows(fields, LANES))
    tile_row = lax.broadcasted_iota(jnp.int32, (tiles, LANES), 0).astype(jnp.float32)
    spans = [jnp.broadcast_to(across[k : k + 1, :], (tiles, LANES)) for k in range(2 * picks)]
    exists = lax.broadcasted_iota(jnp.int32, (tiles, LANES), 1) < group_exp
    for n in range(mats):
        hits = jnp.zeros((group_exp, LANES), jnp.float32)
        spread = jnp.zeros((tiles, LANES), jnp.float32)
        for k in range(picks):
            hits = hits + jnp.where((columns[picks + k] == n) & (columns[k] == tile_lane), 1.0, 0.0)
            spread = spread + jnp.where((spans[picks + k] == n) & (spans[k] == tile_row) & exists, 1.0, 0.0)
        pick_f[n * group_exp : (n + 1) * group_exp, :] = hits.astype(jnp.bfloat16)
        pick_b[n * tiles : (n + 1) * tiles, :] = spread.astype(jnp.bfloat16)
    for e in range(group_exp):
        kern = info[e : e + 1, LANES:]
        ahead = jnp.broadcast_to(kern, (LANES, 2 * LANES))
        band_f[e] = pltpu.roll(ahead, 0, 1, stride=1, stride_axis=0).astype(jnp.bfloat16)
        moved = jnp.broadcast_to(pltpu.roll(kern, 2 * LANES - 2 * PAD, 1), (2 * LANES, 2 * LANES))
        band_b[e] = pltpu.roll(moved, 0, 1, stride=1, stride_axis=0)[:, :LANES].astype(jnp.bfloat16)

    for j in range(1, n_exp):
        slot = lax.rem(x + j, n_exp)
        arrive(obs.at[slot], obs_recv.at[slot])
    loads[7].wait()

    for step in range(ITERS):
        arrive(win.at[step, pl.ds(n_exp, n_exp)], hop_recv.at[step])
        for t in range(tiles):
            put(wide, t * padded, win[step, t].astype(jnp.float32))
        for r in range(rows):
            line = every(wide, r, tiles, padded).astype(jnp.bfloat16)
            mix = dot(pick_f[:, :tiles], line, NN).astype(jnp.bfloat16)
            for n in range(mats):
                mixed[n, r * group_exp : (r + 1) * group_exp, :] = mix[n * group_exp : (n + 1) * group_exp]
        total = dot(mixed[0], table[0], NN)
        for n in range(1, mats):
            total = total + dot(mixed[n], table[n], NN)
        put(pre, 0, total)

        for d in range(n_exp):
            for k in range(count):
                e = d * count + k
                line = pad_rows(every(pre, e, rows, group_exp), padded)
                residual = obs[d, k].astype(jnp.float32) - banded(line, band_f[e], NT)
                if step == ITERS - 1:
                    res_stage[d, k] = residual.astype(jnp.bfloat16)
                put(back, e * padded, banded(residual, band_b[e], NN))
        if step == ITERS - 1:
            res_in[x] = res_stage[x]
            for j in range(1, n_exp):
                peer = lax.rem(x + j, n_exp)
                send(res_stage.at[peer], res_in.at[x], res_send.at[j], res_recv.at[x], (g, peer))

        for r in range(rows):
            line = every(back, r, group_exp, padded).astype(jnp.bfloat16)
            fold = dot(pick_b[:, :group_exp], line, NN)
            for n in range(mats):
                folded[n, r * tiles : (r + 1) * tiles, :] = fold[n * tiles : (n + 1) * tiles]
        total = dot(folded[0].astype(jnp.bfloat16), table[0], NT)
        for n in range(1, mats):
            total = total + dot(folded[n].astype(jnp.bfloat16), table[n], NT)
        put(grad, 0, total)

        for t in range(n_exp):
            line = pad_rows(every(grad, n_exp + t, rows, tiles), padded)
            grad_out[step, t] = line.astype(jnp.bfloat16)
        send(grad_out.at[step], grad_in.at[step], grad_send.at[step], grad_recv.at[step], (after, x))
        arrive(grad_in.at[step], grad_recv.at[step])
        for t in range(n_exp):
            line = pad_rows(every(grad, t, rows, tiles), padded)
            update = STEP * (line + grad_in[step, t].astype(jnp.float32))
            if step < ITERS - 1:
                state[t] = state[t] + update
                delta[t] = delta[t] + update
                win[step + 1, t] = state[t].astype(jnp.bfloat16)
            else:
                delta_stage[t] = (delta[t] + update).astype(jnp.bfloat16)
        if step < ITERS - 1:
            hop(step + 1)

    delta_in[x] = delta_stage[x]
    for j in range(1, n_exp):
        peer = lax.rem(x + j, n_exp)
        send(delta_stage.at[peer], delta_in.at[x], delta_send.at[j], delta_recv.at[x], (g, peer))
    for j in range(1, n_exp):
        slot = lax.rem(x + j, n_exp)
        arrive(res_in.at[slot], res_recv.at[slot])
    for p in range(n_exp):
        span = slice(p * rows, (p + 1) * rows)
        for e in range(count):
            resid_out[e, span, :] = res_in[p, e].astype(jnp.float32)[:rows]
    for j in range(1, n_exp):
        slot = lax.rem(x + j, n_exp)
        arrive(delta_in.at[slot], delta_recv.at[slot])
    for p in range(n_exp):
        span = slice(p * rows, (p + 1) * rows)
        sky_out[span, :] = sky_ref[span, :] + delta_in[p].astype(jnp.float32)[:rows]
    for copy in pending:
        copy.wait_send()


def shards(
    n_grp, n_exp, sky, observed, intersections, resample_index, psf_index, resample_table, psf_weights, psf_basis
):
    bands, lines, width = sky.shape[1:]
    count = intersections.shape[0]
    flat = bands * lines
    rows = flat // n_exp
    padded = -(-rows // 16) * 16
    group_exp = count * n_exp
    tiles = 2 * n_exp
    mats = resample_table.shape[0]
    comp = psf_basis.shape[0]
    operands = (
        intersections, resample_index, psf_index, psf_weights.T, psf_basis,
        sky.reshape(flat, width), observed.reshape(count, flat, width), resample_table,
    )
    vmem = pl.BlockSpec(memory_space=pltpu.VMEM)
    half, full = jnp.bfloat16, jnp.float32
    sems = pltpu.SemaphoreType.DMA
    scratch = [
        *((pltpu.SMEM if i < 4 else pltpu.VMEM)(operand.shape, operand.dtype) for i, operand in enumerate(operands)),
        sems((len(operands),)),
        pltpu.VMEM((n_exp, padded, width), half),
        pltpu.VMEM((n_exp, count, padded, width), half),
        pltpu.VMEM((n_exp, 8, 3 * LANES), full),
        pltpu.VMEM((ITERS, tiles, padded, width), half),
        pltpu.VMEM((n_exp, count, padded, width), half),
        pltpu.VMEM((8, LANES), full),
        pltpu.VMEM((ITERS, n_exp, padded, width), half),
        pltpu.VMEM((ITERS, n_exp, padded, width), half),
        pltpu.VMEM((n_exp, padded, width), half),
        pltpu.VMEM((n_exp, padded, width), half),
        pltpu.VMEM((n_exp, count, padded, width), half),
        pltpu.VMEM((n_exp, count, padded, width), half),
        pltpu.VMEM((comp, 2 * LANES), full),
        pltpu.VMEM((width // LANES, tiles * padded, LANES), full),
        pltpu.VMEM((mats, rows * group_exp, width), half),
        pltpu.VMEM((width // LANES, rows * group_exp, LANES), full),
        pltpu.VMEM((width // LANES, group_exp * padded, LANES), full),
        pltpu.VMEM((mats, rows * tiles, width), full),
        pltpu.VMEM((width // LANES, rows * tiles, LANES), full),
        pltpu.VMEM((n_exp, padded, width), full),
        pltpu.VMEM((n_exp, padded, width), full),
        pltpu.VMEM((mats * group_exp, LANES), half),
        pltpu.VMEM((mats * tiles, LANES), half),
        pltpu.VMEM((group_exp, LANES, 2 * LANES), half),
        pltpu.VMEM((group_exp, 2 * LANES, LANES), half),
        *([sems((n_exp,))] * 6),
        *([sems((ITERS,))] * 4),
        *([sems((n_exp,))] * 4),
    ]
    sky_out, residual = pl.pallas_call(
        functools.partial(kernel, n_grp, n_exp),
        out_shape=(
            jax.ShapeDtypeStruct((flat, width), full),
            jax.ShapeDtypeStruct((count, flat, width), full),
        ),
        in_specs=[pl.BlockSpec(memory_space=pltpu.HBM)] * len(operands),
        out_specs=(vmem, vmem),
        scratch_shapes=scratch,
        compiler_params=pltpu.CompilerParams(
            collective_id=0, has_side_effects=True, vmem_limit_bytes=64 * 2**20
        ),
    )(*operands)
    return sky_out.reshape(sky.shape), residual.reshape(observed.shape)


def solution(mesh):
    both = ("grp", "exp")
    in_specs = (
        P(both, None, None, None), P(both, None, None, None), P(both, None), P(both, None), P(both), P(), P(), P(),
    )
    out_specs = (P(both, None, None, None), P(both, None, None, None))
    body = functools.partial(shards, mesh.shape["grp"], mesh.shape["exp"])
    return jax.shard_map(body, mesh=mesh, in_specs=in_specs, out_specs=out_specs, check_vma=False)
```

time: 52.3 us -> 45.1 us (0.86)
  local copies, waits for them, and re-layouts: 8.86 us -> 3.31 us
  Pallas kernels: 42.4 us -> 41 us
    unnamed x17 -> x2, local copies, waits for them, and re-layouts: 8.86 us -> 3.31 us
    pallas_call x1, Pallas kernels: 42.4 us -> 41 us  [shards(): pl.pallas_call(functools.partial(kernel, n_grp, n_exp), out_shape=(jax.Sh...]
where the time goes in v2:
time: 45.1 us; the launch traced here: 44.9 us
  Pallas kernels  41 us (91%)
  local copies, waits for them, and re-layouts  3.31 us (7%)
  between operations  0.64 us (1%)
    pallas_call x1, Pallas kernels, shards(): pl.pallas_call(functools.partial(kernel, n_grp, n_exp), out_shape=(jax.Sh...  41 us
    unnamed x2, local copies, waits for them, and re-layouts  3.31 us

profile of v2, /device:TPU:0, one launch (start us, length us, event | category | flops | bytes accessed | tf_op | source)
XLA Modules:
  0.0 44.9 jit_solution(9332941955489095627)
XLA Ops:
  0.6 41.0 %shard_map.95 = (f32[48,512]{1,0:T(8,128)}, f32[4,48,512]{2,1,0:T(8,128)}) custom-call(s32[4,4]{1,0:T(4,128)} %refs_0_.1, s32[4,4]{1,0:T(4,128)} %refs_1_.1, s32[4]{0:T(128)} %refs_2_.1, f32[8,16]{1,0:T(8,128)} %bitcast.9, f32[8,41]{1,0:T(8,128)} %refs_4_.1, f32[48,512]{1,0:T(8,128)} %bitcast.8, bf16[4,48,512]{2,1,0:T(8,128)(2,1)} %bitcast.6, ...), custom_call_target="tpu_custom_call" | custom-call | tf_op jit(solution)/shard_map/pallas_call | solution.py:302
  41.6 1.5 %copy.12 = f32[1,6,8,512]{3,2,1,0:T(8,128)} copy(f32[1,6,8,512]{3,2,1,0:T(8,128)} %bitcast.7) | data formatting | bytes 196608
  43.2 1.8 %copy.13 = f32[4,6,8,512]{3,2,1,0:T(8,128)} copy(f32[4,6,8,512]{3,2,1,0:T(8,128)} %bitcast.5) | data formatting | bytes 786432

commit v3 on v2

--- a/solution.py
+++ b/solution.py
@@ -52,7 +52,8 @@
     (load_sem, sky_stage, obs_stage, meta, win, obs, back_in, grad_in, grad_out, delta_stage, delta_in,
      res_stage, res_in, taps, wide, mixed, pre, back, folded, grad, state, delta, pick_f, pick_b, band_f, band_b,
      sky_send, sky_recv, meta_send, meta_recv, obs_send, obs_recv, hop_send, hop_recv, grad_send, grad_recv,
-     delta_send, delta_recv, res_send, res_recv) = rest
+     delta_send, delta_recv, res_send, res_recv,
+     next_send, next_recv, last_send, last_recv, last_stage, last_in) = rest
     g = lax.axis_index("grp")
     x = lax.axis_index("exp")
     before = lax.rem(g + n_grp - 1, n_grp)
@@ -72,10 +73,10 @@
         loads[i].start()
 
     barrier = pltpu.get_barrier_semaphore()
-    for j in range(1, n_exp):
-        pl.semaphore_signal(barrier, inc=1, device_id=(g, lax.rem(x + j, n_exp)), device_id_type=MESH)
-    for group in (before, after):
-        pl.semaphore_signal(barrier, inc=1, device_id=(group, x), device_id_type=MESH)
+    for j in range(n_exp):
+        peer = lax.rem(x + j, n_exp)
+        for group in (before, after, g) if j else (before, after):
+            pl.semaphore_signal(barrier, inc=1, device_id=(group, peer), device_id_type=MESH)
 
     def send(src, dst, send_sem, recv_sem, where):
         copy = pltpu.make_async_remote_copy(
@@ -92,7 +93,10 @@
     for p in range(n_exp):
         sky_stage[p] = pad_rows(sky_ref[p * rows : (p + 1) * rows, :], padded).astype(jnp.bfloat16)
     win[0, x] = sky_stage[x]
-    pl.semaphore_wait(barrier, n_exp + 1)
+    pl.semaphore_wait(barrier, 3 * n_exp - 1)
+    for j in range(n_exp):
+        peer = lax.rem(x + j, n_exp)
+        send(sky_stage.at[peer], win.at[0, n_exp + x], next_send.at[j], next_recv.at[x], (before, peer))
     for j in range(1, n_exp):
         peer = lax.rem(x + j, n_exp)
         send(sky_stage.at[peer], win.at[0, x], sky_send.at[j], sky_recv.at[x], (g, peer))
@@ -126,20 +130,6 @@
     for j in range(1, n_exp):
         peer = lax.rem(x + j, n_exp)
         send(obs_stage.at[peer], obs.at[x], obs_send.at[j], obs_recv.at[x], (g, peer))
-
-    def hop(step):
-        send(
-            win.at[step, pl.ds(0, n_exp)], win.at[step, pl.ds(n_exp, n_exp)], hop_send.at[step], hop_recv.at[step],
-            (before, x),
-        )
-
-    for j in range(1, n_exp):
-        slot = lax.rem(x + j, n_exp)
-        arrive(win.at[0, slot], sky_recv.at[slot])
-    hop(0)
-    for t in range(n_exp):
-        state[t] = win[0, t].astype(jnp.float32)
-        delta[t] = jnp.zeros_like(state[t])
 
     for j in range(1, n_exp):
         slot = lax.rem(x + j, n_exp)
@@ -171,11 +161,19 @@
         slot = lax.rem(x + j, n_exp)
         arrive(obs.at[slot], obs_recv.at[slot])
     loads[7].wait()
+    for j in range(1, n_exp):
+        slot = lax.rem(x + j, n_exp)
+        arrive(win.at[0, slot], sky_recv.at[slot])
+    for j in range(n_exp):
+        arrive(win.at[0, n_exp + j], next_recv.at[j])
+    for t in range(tiles):
+        state[t] = win[0, t].astype(jnp.float32)
+    for t in range(n_exp):
+        delta[t] = jnp.zeros_like(state[t])
 
     for step in range(ITERS):
-        arrive(win.at[step, pl.ds(n_exp, n_exp)], hop_recv.at[step])
         for t in range(tiles):
-            put(wide, t * padded, win[step, t].astype(jnp.float32))
+            put(wide, t * padded, state[t])
         for r in range(rows):
             line = every(wide, r, tiles, padded).astype(jnp.bfloat16)
             mix = dot(pick_f[:, :tiles], line, NN).astype(jnp.bfloat16)
@@ -210,23 +208,28 @@
             total = total + dot(folded[n].astype(jnp.bfloat16), table[n], NT)
         put(grad, 0, total)
 
-        for t in range(n_exp):
-            line = pad_rows(every(grad, n_exp + t, rows, tiles), padded)
-            grad_out[step, t] = line.astype(jnp.bfloat16)
-        send(grad_out.at[step], grad_in.at[step], grad_send.at[step], grad_recv.at[step], (after, x))
-        arrive(grad_in.at[step], grad_recv.at[step])
-        for t in range(n_exp):
-            line = pad_rows(every(grad, t, rows, tiles), padded)
-            update = STEP * (line + grad_in[step, t].astype(jnp.float32))
-            if step < ITERS - 1:
+        parts = [pad_rows(every(grad, t, rows, tiles), padded) for t in range(tiles)]
+        if step < ITERS - 1:
+            for t in range(tiles):
+                grad_out[step, t] = parts[t].astype(jnp.bfloat16)
+            own, following = pl.ds(0, n_exp), pl.ds(n_exp, n_exp)
+            send(grad_out.at[step, following], grad_in.at[step, own], grad_send.at[step], grad_recv.at[step], (after, x))
+            send(grad_out.at[step, own], grad_in.at[step, following], hop_send.at[step], hop_recv.at[step], (before, x))
+            arrive(grad_in.at[step, own], grad_recv.at[step])
+            arrive(grad_in.at[step, following], hop_recv.at[step])
+            for t in range(tiles):
+                update = STEP * (parts[t] + grad_in[step, t].astype(jnp.float32))
                 state[t] = state[t] + update
-                delta[t] = delta[t] + update
-                win[step + 1, t] = state[t].astype(jnp.bfloat16)
-            else:
-                delta_stage[t] = (delta[t] + update).astype(jnp.bfloat16)
-        if step < ITERS - 1:
-            hop(step + 1)
-
+                if t < n_exp:
+                    delta[t] = delta[t] + update
+        else:
+            for t in range(n_exp):
+                last_stage[t] = (STEP * parts[n_exp + t]).astype(jnp.bfloat16)
+                delta_stage[t] = (delta[t] + STEP * parts[t]).astype(jnp.bfloat16)
+
+    for j in range(n_exp):
+        peer = lax.rem(x + j, n_exp)
+        send(last_stage.at[peer], last_in.at[x], last_send.at[j], last_recv.at[x], (after, peer))
     delta_in[x] = delta_stage[x]
     for j in range(1, n_exp):
         peer = lax.rem(x + j, n_exp)
@@ -241,9 +244,11 @@
     for j in range(1, n_exp):
         slot = lax.rem(x + j, n_exp)
         arrive(delta_in.at[slot], delta_recv.at[slot])
+    for j in range(n_exp):
+        arrive(last_in.at[j], last_recv.at[j])
     for p in range(n_exp):
         span = slice(p * rows, (p + 1) * rows)
-        sky_out[span, :] = sky_ref[span, :] + delta_in[p].astype(jnp.float32)[:rows]
+        sky_out[span, :] = sky_ref[span, :] + (delta_in[p].astype(jnp.float32) + last_in[p].astype(jnp.float32))[:rows]
     for copy in pending:
         copy.wait_send()
 
@@ -273,11 +278,11 @@
         pltpu.VMEM((n_exp, padded, width), half),
         pltpu.VMEM((n_exp, count, padded, width), half),
         pltpu.VMEM((n_exp, 8, 3 * LANES), full),
-        pltpu.VMEM((ITERS, tiles, padded, width), half),
+        pltpu.VMEM((1, tiles, padded, width), half),
         pltpu.VMEM((n_exp, count, padded, width), half),
         pltpu.VMEM((8, LANES), full),
-        pltpu.VMEM((ITERS, n_exp, padded, width), half),
-        pltpu.VMEM((ITERS, n_exp, padded, width), half),
+        pltpu.VMEM((ITERS, tiles, padded, width), half),
+        pltpu.VMEM((ITERS, tiles, padded, width), half),
         pltpu.VMEM((n_exp, padded, width), half),
         pltpu.VMEM((n_exp, padded, width), half),
         pltpu.VMEM((n_exp, count, padded, width), half),
@@ -289,7 +294,7 @@
         pltpu.VMEM((width // LANES, group_exp * padded, LANES), full),
         pltpu.VMEM((mats, rows * tiles, width), full),
         pltpu.VMEM((width // LANES, rows * tiles, LANES), full),
-        pltpu.VMEM((n_exp, padded, width), full),
+        pltpu.VMEM((tiles, padded, width), full),
         pltpu.VMEM((n_exp, padded, width), full),
         pltpu.VMEM((mats * group_exp, LANES), half),
         pltpu.VMEM((mats * tiles, LANES), half),
@@ -297,7 +302,8 @@
         pltpu.VMEM((group_exp, 2 * LANES, LANES), half),
         *([sems((n_exp,))] * 6),
         *([sems((ITERS,))] * 4),
-        *([sems((n_exp,))] * 4),
+        *([sems((n_exp,))] * 8),
+        *([pltpu.VMEM((n_exp, padded, width), half)] * 2),
     ]
     sky_out, residual = pl.pallas_call(
         functools.partial(kernel, n_grp, n_exp),

time: 45.1 us -> 39.3 us (0.87)
  Pallas kernels: 41 us -> 35.1 us
    pallas_call x1, Pallas kernels: 41 us -> 35.1 us  [shards(): pl.pallas_call(functools.partial(kernel, n_grp, n_exp), out_shape=(jax.Sh...]
where the time goes in v3:
time: 39.3 us; the launch traced here: 39.1 us
  Pallas kernels  35.1 us (89%)
  local copies, waits for them, and re-layouts  3.31 us (8%)
  between operations  0.64 us (2%)
    pallas_call x1, Pallas kernels, shards(): pl.pallas_call(functools.partial(kernel, n_grp, n_exp), out_shape=(jax.Sh...  35.1 us
    unnamed x2, local copies, waits for them, and re-layouts  3.31 us

profile of v3, /device:TPU:0, one launch (start us, length us, event | category | flops | bytes accessed | tf_op | source)
XLA Modules:
  0.0 39.1 jit_solution(15265792096978524278)
XLA Ops:
  0.6 35.1 %shard_map.95 = (f32[48,512]{1,0:T(8,128)}, f32[4,48,512]{2,1,0:T(8,128)}) custom-call(s32[4,4]{1,0:T(4,128)} %refs_0_.1, s32[4,4]{1,0:T(4,128)} %refs_1_.1, s32[4]{0:T(128)} %refs_2_.1, f32[8,16]{1,0:T(8,128)} %bitcast.9, f32[8,41]{1,0:T(8,128)} %refs_4_.1, f32[48,512]{1,0:T(8,128)} %bitcast.8, bf16[4,48,512]{2,1,0:T(8,128)(2,1)} %bitcast.6, ...), custom_call_target="tpu_custom_call" | custom-call | tf_op jit(solution)/shard_map/pallas_call | solution.py:308
  35.8 1.5 %copy.12 = f32[1,6,8,512]{3,2,1,0:T(8,128)} copy(f32[1,6,8,512]{3,2,1,0:T(8,128)} %bitcast.7) | data formatting | bytes 196608
  37.3 1.8 %copy.13 = f32[4,6,8,512]{3,2,1,0:T(8,128)} copy(f32[4,6,8,512]{3,2,1,0:T(8,128)} %bitcast.5) | data formatting | bytes 786432

commit v4 on v3

--- a/solution.py
+++ b/solution.py
@@ -93,14 +93,6 @@
     for p in range(n_exp):
         sky_stage[p] = pad_rows(sky_ref[p * rows : (p + 1) * rows, :], padded).astype(jnp.bfloat16)
     win[0, x] = sky_stage[x]
-    pl.semaphore_wait(barrier, 3 * n_exp - 1)
-    for j in range(n_exp):
-        peer = lax.rem(x + j, n_exp)
-        send(sky_stage.at[peer], win.at[0, n_exp + x], next_send.at[j], next_recv.at[x], (before, peer))
-    for j in range(1, n_exp):
-        peer = lax.rem(x + j, n_exp)
-        send(sky_stage.at[peer], win.at[0, x], sky_send.at[j], sky_recv.at[x], (g, peer))
-
     for i in (0, 1, 2, 3, 4):
         loads[i].wait()
     taps[...] = jnp.zeros_like(taps)
@@ -117,9 +109,6 @@
             kern = kern + weights_smem[c, psf_smem[e]] * taps[c : c + 1, :]
         info.append(jnp.concatenate([fields, kern], axis=1))
     meta[x] = pad_rows(jnp.concatenate(info, axis=0), meta.shape[1])
-    for j in range(1, n_exp):
-        peer = lax.rem(x + j, n_exp)
-        send(meta.at[x], meta.at[x], meta_send.at[j], meta_recv.at[x], (g, peer))
 
     loads[6].wait()
     for e in range(count):
@@ -127,6 +116,16 @@
         for p in range(n_exp):
             obs_stage[p, e] = pad_rows(whole[p * rows : (p + 1) * rows, :], padded).astype(jnp.bfloat16)
     obs[x] = obs_stage[x]
+    pl.semaphore_wait(barrier, 3 * n_exp - 1)
+    for j in range(n_exp):
+        peer = lax.rem(x + j, n_exp)
+        send(sky_stage.at[peer], win.at[0, n_exp + x], next_send.at[j], next_recv.at[x], (before, peer))
+    for j in range(1, n_exp):
+        peer = lax.rem(x + j, n_exp)
+        send(sky_stage.at[peer], win.at[0, x], sky_send.at[j], sky_recv.at[x], (g, peer))
+    for j in range(1, n_exp):
+        peer = lax.rem(x + j, n_exp)
+        send(meta.at[x], meta.at[x], meta_send.at[j], meta_recv.at[x], (g, peer))
     for j in range(1, n_exp):
         peer = lax.rem(x + j, n_exp)
         send(obs_stage.at[peer], obs.at[x], obs_send.at[j], obs_recv.at[x], (g, peer))

time: 39.3 us -> 39.2 us (level)
  no operation moved by 1% of the time
where the time goes in v4:
time: 39.2 us; the launch traced here: 39.1 us
  Pallas kernels  35.1 us (90%)
  local copies, waits for them, and re-layouts  3.31 us (8%)
  between operations  0.64 us (2%)
    pallas_call x1, Pallas kernels, shards(): pl.pallas_call(functools.partial(kernel, n_grp, n_exp), out_shape=(jax.Sh...  35.1 us
    unnamed x2, local copies, waits for them, and re-layouts  3.31 us

profile of v4, /device:TPU:0, one launch (start us, length us, event | category | flops | bytes accessed | tf_op | source)
XLA Modules:
  0.0 39.1 jit_solution(11241521688025123625)
XLA Ops:
  0.6 35.1 %shard_map.95 = (f32[48,512]{1,0:T(8,128)}, f32[4,48,512]{2,1,0:T(8,128)}) custom-call(s32[4,4]{1,0:T(4,128)} %refs_0_.1, s32[4,4]{1,0:T(4,128)} %refs_1_.1, s32[4]{0:T(128)} %refs_2_.1, f32[8,16]{1,0:T(8,128)} %bitcast.9, f32[8,41]{1,0:T(8,128)} %refs_4_.1, f32[48,512]{1,0:T(8,128)} %bitcast.8, bf16[4,48,512]{2,1,0:T(8,128)(2,1)} %bitcast.6, ...), custom_call_target="tpu_custom_call" | custom-call | tf_op jit(solution)/shard_map/pallas_call | solution.py:307
  35.8 1.5 %copy.12 = f32[1,6,8,512]{3,2,1,0:T(8,128)} copy(f32[1,6,8,512]{3,2,1,0:T(8,128)} %bitcast.7) | data formatting | bytes 196608
  37.3 1.8 %copy.13 = f32[4,6,8,512]{3,2,1,0:T(8,128)} copy(f32[4,6,8,512]{3,2,1,0:T(8,128)} %bitcast.5) | data formatting | bytes 786432
